TPU v7x, 256 devices: a whole 4x4x8 slice. The times are simulated.
256 devices in a mesh: section: 2 (over z_lo), fsdp: 32 (over z_hi, y, core), tensor: 4 (over x).
Axes of the slice: x: 4, y: 4, z: 8 (z_hi: 4, z_lo: 2; z = z_hi * 2 + z_lo), core: 2. Of those that a mesh axis runs over, the one named last changes fastest.
Arguments:
- frames: bfloat16 [4096, 3072], P('fsdp', 'tensor')
- lengths: int32 [32], P('fsdp'), may hold values from 16 to 128, as said below
- qkv_weight: bfloat16 [2, 3, 3072, 1536], P('section', None, 'fsdp', 'tensor'), as said below
- out_weight: bfloat16 [2, 1536, 3072], P('section', 'tensor', 'fsdp'), may hold values from -0.15625 to 0.15625
- grad_out: bfloat16 [4096, 3072], P('fsdp', 'tensor'), may hold values from -6 to 6
Outputs:
- input_grads: bfloat16 [2, 4096, 3072], P('section', 'fsdp', 'tensor')
- qkv_grad: bfloat16 [2, 3, 3072, 1536], P('section', None, 'fsdp', 'tensor')
- out_grad: bfloat16 [2, 1536, 3072], P('section', 'tensor', 'fsdp')
Inputs may be any that keep to these rules, and one draw needn't show every extreme that they name: Utterance b's live frames are its first lengths[b] slots; some utterance fills all 128 slots. `qkv_weight`: index 0, 1, 2 of the second dimension are the query, key and value projections.
All inputs are finite; a program needn't handle non-finite values.
Results may differ from a plain program's by a relative error of at most 0.03.
Values may be sent and summed in bfloat16 or wider, within the bound.
No kernel may reach another device: no remote copies, remote signals or barrier semaphores. Data moves between devices by JAX's collectives and lax.ppermute only.
A program may use at most 64 MiB of HBM per device.

v0:
```python
import jax
import jax.numpy as jnp
from jax import lax
from jax.sharding import PartitionSpec as P

HEAD = 128
EPSILON = 1e-05


def from_behind(value, axis, steps):
    count = lax.axis_size(axis)
    leading, last = (max(0, -steps), min(count, count - steps))
    return lax.ppermute(value, axis, [(source, source + steps) for source in range(leading, last)])


def attend_forward(queries, key_rows, values, live_keys):
    score_scale = float(HEAD) ** (-0.5)
    scores = (
        jnp.einsum("bqhe,bkhe->bhqk", queries, key_rows, preferred_element_type=jnp.float32)
        * score_scale
    )
    scores = jnp.where(live_keys[:, None, None, :], scores, jnp.float32(-1e30))
    highest = jnp.max(scores, axis=-1, keepdims=True)
    raised = jnp.exp(scores - highest)
    attend = raised / jnp.sum(raised, axis=-1, keepdims=True)
    attend_low = attend.astype(jnp.bfloat16)
    context = jnp.einsum(
        "bhqk,bkhe->bqhe", attend_low, values, preferred_element_type=jnp.float32
    ).astype(jnp.bfloat16)
    return (attend, attend_low, context)


def layer_forward(hidden_own, w_qkv, w_out, live_keys, live_rows):
    whole = lax.all_gather(hidden_own, "tensor", axis=1, tiled=True)
    widened = whole.astype(jnp.float32)
    average = jnp.mean(widened, axis=-1, keepdims=True)
    centered = widened - average
    variance = jnp.mean(centered * centered, axis=-1, keepdims=True)
    inverse = lax.rsqrt(variance + EPSILON)
    unit_rows = centered * inverse
    normed = unit_rows.astype(jnp.bfloat16)
    projected = jnp.einsum("rd,cdh->crh", normed, w_qkv, preferred_element_type=jnp.float32).astype(
        jnp.bfloat16
    )
    utterances, length = live_keys.shape
    split_qkv = projected.reshape(3, utterances, length, -1, HEAD)
    attend, attend_low, context = attend_forward(
        split_qkv[0], split_qkv[1], split_qkv[2], live_keys
    )
    context = context.reshape(utterances * length, -1)
    mixed = jnp.dot(context, w_out, preferred_element_type=jnp.float32)
    mixed_own = lax.psum_scatter(mixed, "tensor", scatter_dimension=1, tiled=True)
    output = (hidden_own.astype(jnp.float32) + live_rows * mixed_own).astype(jnp.bfloat16)
    return (output, (unit_rows, inverse, normed, split_qkv, attend, attend_low, context))


def layer_backward(grad_own, kept_state, w_qkv, w_out, live_rows):
    unit_rows, inverse, normed, split_qkv, attend, attend_low, context = kept_state
    score_scale = float(HEAD) ** (-0.5)
    whole_grad = lax.all_gather(grad_own, "tensor", axis=1, tiled=True)
    masked = (live_rows * whole_grad.astype(jnp.float32)).astype(jnp.bfloat16)
    grad_context = jnp.einsum(
        "rd,hd->rh", masked, w_out, preferred_element_type=jnp.float32
    ).astype(jnp.bfloat16)
    grad_context = grad_context.reshape(split_qkv.shape[1:])
    queries, key_rows, values = (split_qkv[0], split_qkv[1], split_qkv[2])
    grad_attend = jnp.einsum(
        "bqhe,bkhe->bhqk", grad_context, values, preferred_element_type=jnp.float32
    )
    grad_values = jnp.einsum(
        "bhqk,bqhe->bkhe", attend_low, grad_context, preferred_element_type=jnp.float32
    ).astype(jnp.bfloat16)
    inner = jnp.sum(grad_attend * attend, axis=-1, keepdims=True)
    grad_scores = (attend * (grad_attend - inner) * score_scale).astype(jnp.bfloat16)
    grad_queries = jnp.einsum(
        "bhqk,bkhe->bqhe", grad_scores, key_rows, preferred_element_type=jnp.float32
    ).astype(jnp.bfloat16)
    grad_keys = jnp.einsum(
        "bhqk,bqhe->bkhe", grad_scores, queries, preferred_element_type=jnp.float32
    ).astype(jnp.bfloat16)
    frame_rows, own_width = grad_own.shape
    grad_qkv = jnp.stack([grad_queries, grad_keys, grad_values]).reshape(3, frame_rows, -1)
    norm_part = jnp.einsum("crh,cdh->rd", grad_qkv, w_qkv, preferred_element_type=jnp.float32)
    first_col = lax.axis_index("tensor") * own_width
    norm_grad = lax.psum(norm_part.astype(jnp.bfloat16), "tensor").astype(jnp.float32)
    centered = (
        norm_grad
        - jnp.mean(norm_grad, axis=-1, keepdims=True)
        - unit_rows * jnp.mean(norm_grad * unit_rows, axis=-1, keepdims=True)
    )
    centered_own = lax.dynamic_slice_in_dim(centered, first_col, own_width, 1)
    grad_in = (grad_own.astype(jnp.float32) + inverse * centered_own).astype(jnp.bfloat16)
    return (grad_in, masked, grad_qkv)


def local(frames, lengths, qkv_weight, out_weight, grad_out):
    frame_rows = frames.shape[0]
    utterances = lengths.shape[0]
    length = frame_rows // utterances
    live_keys = jnp.arange(length, dtype=jnp.int32)[None, :] < lengths[:, None]
    live_rows = live_keys.reshape(frame_rows, 1).astype(jnp.float32)
    gathered = (
        lax.all_gather(qkv_weight, "fsdp", axis=2, tiled=True),
        lax.all_gather(out_weight, "fsdp", axis=2, tiled=True),
    )
    w_qkv = gathered[0][0]
    w_out = gathered[1][0]
    first_out, _ = layer_forward(frames, w_qkv, w_out, live_keys, live_rows)
    arrived = from_behind(first_out, "section", 1)
    on_first = lax.axis_index("section") == 0
    entry = jnp.where(on_first, frames, arrived)
    _, kept_state = layer_forward(entry, w_qkv, w_out, live_keys, live_rows)
    upper_grad, _, _ = layer_backward(grad_out, kept_state, w_qkv, w_out, live_rows)
    returned = from_behind(upper_grad, "section", -1)
    top_grad = jnp.where(on_first, returned, grad_out)
    grad_in, masked, grad_qkv = layer_backward(top_grad, kept_state, w_qkv, w_out, live_rows)
    normed = kept_state[2]
    context = kept_state[6]
    full_width = normed.shape[1]
    head_width = context.shape[1]
    term_qkv = jnp.einsum(
        "rd,crh->dch", normed, grad_qkv, preferred_element_type=jnp.float32
    ).reshape(full_width, 3 * head_width)
    term_out = jnp.einsum("rd,rh->dh", masked, context, preferred_element_type=jnp.float32)
    summed = lax.psum_scatter(
        jnp.concatenate([term_qkv, term_out], axis=1).astype(jnp.bfloat16),
        "fsdp",
        scatter_dimension=0,
        tiled=True,
    ).astype(jnp.float32)
    own_rows = summed.shape[0]
    qkv_grad = (
        summed[:, : 3 * head_width]
        .reshape(own_rows, 3, head_width)
        .transpose(1, 0, 2)[None]
        .astype(jnp.bfloat16)
    )
    out_grad = summed[:, 3 * head_width :].T[None].astype(jnp.bfloat16)
    return (grad_in[None], qkv_grad, out_grad)


def solution(mesh):
    in_specs = (
        P("fsdp", "tensor"),
        P("fsdp"),
        P("section", None, "fsdp", "tensor"),
        P("section", "tensor", "fsdp"),
        P("fsdp", "tensor"),
    )
    out_specs = (
        P("section", "fsdp", "tensor"),
        P("section", None, "fsdp", "tensor"),
        P("section", "tensor", "fsdp"),
    )
    return jax.shard_map(local, mesh=mesh, in_specs=in_specs, out_specs=out_specs, check_vma=False)
```

profile of v0, /device:TPU:1, one launch (start us, length us, event | category | flops | bytes accessed | tf_op | source)
XLA Modules:
  0.0 505.9 jit_solution(2395847243303926381)
XLA Ops:
  7.2 0.7 all-gather.3.cloned.1.call-update
  7.9 0.7 all-gather.5.cloned.1.call-update
  9.4 13.1 %all_gather.18 = bf16[128,3072]{1,0:T(8,128)(2,1)S(1)} all-gather(bf16[128,768]{1,0:T(8,128)(2,1)} %param.5), channel_id=1, replica_groups=mesh['section'=2,'fsdp'=32,'tensor'=4] {'tensor'}, dimensions={1}, use_global_device_ids=true | all-gather | bytes 983040 | tf_op jit(solution)/shard_map/all_gather | solution.py:34
  22.7 0.4 fusion.35
  23.1 64.4 %all-gather.3.cloned.1.call-done = bf16[1,3,3072,384]{3,2,1,0:T(8,128)(2,1)} async-done(((bf16[1,3,96,384]{3,2,1,0:T(8,128)(2,1)}), bf16[1,3,3072,384]{3,2,1,0:T(8,128)(2,1)}) %all-gather.3.cloned.1.call-update) | async-done | bytes 7077904 | tf_op jit(solution)/shard_map/all_gather | solution.py:103
  87.4 4.2 fusion.48
  92.1 0.3 fusion.124
  92.4 0.2 fusion.58
  92.6 0.2 convolution_convert_fusion.9
  92.8 50.7 %all-gather.5.cloned.1.call-done = bf16[1,384,3072]{1,2,0:T(8,128)(2,1)} async-done(((bf16[1,384,96]{1,2,0:T(8,128)(2,1)}), bf16[1,384,3072]{1,2,0:T(8,128)(2,1)}) %all-gather.5.cloned.1.call-update) | async-done | bytes 2359312 | tf_op jit(solution)/shard_map/all_gather | solution.py:104
  143.5 3.7 fusion.28
  147.3 0.8 copy-done.6
  148.2 14.8 %all_gather.22 = bf16[128,3072]{1,0:T(8,128)(2,1)S(1)} all-gather(bf16[128,768]{1,0:T(8,128)(2,1)S(1)} %copy-done.6), channel_id=1, replica_groups=mesh['section'=2,'fsdp'=32,'tensor'=4] {'tensor'}, dimensions={1}, use_global_device_ids=true | all-gather | bytes 983040 | tf_op jit(solution)/shard_map/all_gather | solution.py:60
  163.0 11.8 %reduce-scatter.5.cloned.1.call-done = f32[128,768]{1,0:T(8,128)} async-done(((f32[128,3072]{1,0:T(8,128)}), f32[128,768]{1,0:T(8,128)}) %reduce-scatter.5.cloned.1.call-update) | async-done | bytes 393232 | tf_op jit(solution)/shard_map/reduce_scatter | solution.py:52
  174.8 1.8 add_convert_fusion
  176.6 2.0 collective-permute-start
  178.6 1.3 fusion.63
  179.8 1.6 copy.83
  181.5 12.3 %all_gather.21 = bf16[128,3072]{1,0:T(8,128)(2,1)S(1)} all-gather(bf16[128,768]{1,0:T(8,128)(2,1)S(1)} %broadcast_select_fusion.1), channel_id=1, replica_groups=mesh['section'=2,'fsdp'=32,'tensor'=4] {'tensor'}, dimensions={1}, use_global_device_ids=true | all-gather | bytes 983040 | tf_op jit(solution)/shard_map/all_gather | solution.py:34
  194.0 0.4 fusion.34
  194.4 4.2 fusion.45
  198.6 0.7 fusion.122
  199.3 1.0 copy.84
  200.4 1.7 copy.80
  202.0 0.7 copy.79
  202.8 1.8 fusion.126
  204.6 2.5 fusion.125
  207.1 2.1 convolution_convert_fusion.6
  209.1 2.1 convolution_convert_fusion.8
  211.3 2.1 convolution_convert_fusion.7
  213.4 1.0 copy.92
  214.4 1.6 copy.91
  216.0 1.6 copy.90
  217.7 6.4 %fusion.21 = bf16[128,3072]{1,0:T(8,128)(2,1)} fusion(bf16[1,3,3072,384]{3,2,1,0:T(8,128)(2,1)} %all-gather.3.cloned.1.call-done, bf16[1,128,384]{2,1,0:T(8,128)(2,1)S(1)} %copy.92, bf16[1,128,384]{2,1,0:T(8,128)(2,1)} %copy.91, bf16[1,128,384]{2,1,0:T(8,128)(2,1)} %copy.90), kind=kOutput, calls=%fused_computation.18 | convolution fusion | flops 906657792 | bytes 8159232 | tf_op jit(solution)/shard_map/crh,cdh->rd/dot_general | solution.py:83
  224.2 50.4 %all-reduce.3.cloned.1.call-done = bf16[128,3072]{1,0:T(8,128)(2,1)} async-done(((bf16[128,3072]{1,0:T(8,128)(2,1)}), bf16[128,3072]{1,0:T(8,128)(2,1)}) %all-reduce.3.cloned.1.call-update) | async-done | bytes 786448 | tf_op jit(solution)/shard_map/psum | solution.py:85
  274.6 1.8 convert_reduce_fusion.3
  276.6 1.0 fusion.82
  277.6 1.3 collective-permute-start.1
  278.9 1.9 convolution_convert_fusion.2
  280.9 3.5 collective-permute-done.1
  284.3 0.9 broadcast_select_fusion
  285.3 10.7 %all_gather.23 = bf16[128,3072]{1,0:T(8,128)(2,1)S(1)} all-gather(bf16[128,768]{1,0:T(8,128)(2,1)S(1)} %broadcast_select_fusion), channel_id=1, replica_groups=mesh['section'=2,'fsdp'=32,'tensor'=4] {'tensor'}, dimensions={1}, use_global_device_ids=true | all-gather | bytes 983040 | tf_op jit(solution)/shard_map/all_gather | solution.py:60
  295.9 0.9 copy-done.1
  296.8 0.6 fusion.66
  297.6 1.4 convolution_convert_fusion.3
  299.0 0.2 fusion.127
  299.3 1.2 convolution_convert_fusion.5
  300.5 1.3 convolution_convert_fusion.4
  302.2 0.2 copy.102
  302.5 6.3 %fusion.18 = bf16[128,3072]{1,0:T(8,128)(2,1)} fusion(bf16[1,3,3072,384]{3,2,1,0:T(8,128)(2,1)} %all-gather.3.cloned.1.call-done, bf16[1,128,384]{2,1,0:T(8,128)(2,1)S(1)} %copy.101, bf16[1,128,384]{2,1,0:T(8,128)(2,1)S(1)} %copy.100, bf16[1,128,384]{2,1,0:T(8,128)(2,1)S(1)} %copy.99), kind=kOutput, calls=%fused_computation.17 | convolution fusion | flops 906657792 | bytes 8159232 | tf_op jit(solution)/shard_map/crh,cdh->rd/dot_general | solution.py:83
  308.9 0.8 convolution_convert_fusion.1
  309.7 2.1 convolution_convert_fusion
  311.8 10.1 %pad_maximum_fusion = bf16[3072,1536]{0,1:T(8,128)(2,1)} fusion(bf16[3072,384]{0,1:T(8,128)(2,1)S(1)} %convolution_convert_fusion.1, bf16[3072,1152]{0,1:T(8,128)(2,1)S(1)} %convolution_convert_fusion), kind=kLoop, calls=%fused_computation.5 | loop fusion | flops 18874368 | bytes 18874368 | tf_op jit(solution)/shard_map/concatenate | solution.py:126
  322.0 12.7 %copy.122 = bf16[3072,1536]{1,0:T(8,128)(2,1)} copy(bf16[3072,1536]{0,1:T(8,128)(2,1)} %pad_maximum_fusion) | data formatting | bytes 18874368
  334.7 28.0 %all-reduce.5.cloned.1.call-done = bf16[128,3072]{1,0:T(8,128)(2,1)} async-done(((bf16[128,3072]{1,0:T(8,128)(2,1)}), bf16[128,3072]{1,0:T(8,128)(2,1)}) %all-reduce.5.cloned.1.call-update) | async-done | bytes 786448 | tf_op jit(solution)/shard_map/psum | solution.py:85
  362.7 1.4 convert_element_type.235
  364.1 0.6 convert_reduce_fusion.2
  364.7 1.8 fusion.98
  366.5 128.8 %reduce-scatter.7.cloned.1.call-done = bf16[96,1536]{1,0:T(8,128)(2,1)} async-done(((bf16[3072,1536]{1,0:T(8,128)(2,1)}), bf16[96,1536]{1,0:T(8,128)(2,1)}) %reduce-scatter.7.cloned.1.call-update) | async-done | bytes 294928
  495.3 0.9 slice.53
  496.3 0.7 copy.105
  497.0 1.0 slice.52
  498.0 0.2 copy.124
  498.2 0.9 copy.104
  (64 shorter events, 2.0 us)
Async XLA Ops:
  7.2 80.3 %all-gather.3.cloned.1.call-start = ((), (), s32[]{:S(2)}) async-start(), calls=%async_computation.2 | async-start | bytes 7299072 | tf_op jit(solution)/shard_map/all_gather | solution.py:103
  7.9 135.6 %all-gather.5.cloned.1.call-start = ((), (), s32[]{:S(2)}) async-start(), calls=%async_computation.3 | async-start | bytes 2433024 | tf_op jit(solution)/shard_map/all_gather | solution.py:104
  8.6 166.1 %reduce-scatter.5.cloned.1.call-start = ((), (), s32[]{:S(2)}) async-start(), calls=%async_computation.4 | async-start | bytes 1966080 | tf_op jit(solution)/shard_map/reduce_scatter | solution.py:52
  147.2 0.9 copy-start.6
  147.2 27.6 %copy-start.7 = (bf16[128,768]{1,0:T(8,128)(2,1)S(1)}, bf16[128,768]{1,0:T(8,128)(2,1)}, u32[]{:S(2)}) copy-start(bf16[128,768]{1,0:T(8,128)(2,1)} %param.5) | copy-start | bytes 589828
  147.3 31.3 %copy-start = (bf16[1,384,3072]{1,2,0:T(8,128)(2,1)S(1)}, bf16[1,384,3072]{1,2,0:T(8,128)(2,1)}, u32[]{:S(2)}) copy-start(bf16[1,384,3072]{1,2,0:T(8,128)(2,1)} %all-gather.5.cloned.1.call-done) | copy-start | bytes 7077892
  147.3 127.3 %all-reduce.3.cloned.1.call-start = ((), (), s32[]{:S(2)}) async-start(), calls=%async_computation.5 | async-start | bytes 1572864 | tf_op jit(solution)/shard_map/psum | solution.py:85
  176.6 4.9 collective-permute-start
  200.4 78.5 %copy-start.8 = (bf16[1,128,384]{1,2,0:T(8,128)(2,1)}, bf16[1,128,384]{1,2,0:T(8,128)(2,1)S(1)}, u32[]{:S(2)}) copy-start(bf16[1,128,384]{1,2,0:T(8,128)(2,1)S(1)} %copy.84) | copy-start | bytes 294916
  202.8 8.5 %copy-start.11 = (bf16[1,128,384]{1,2,0:T(8,128)(2,1)S(1)}, bf16[1,128,384]{1,2,0:T(8,128)(2,1)}, u32[]{:S(2)}) copy-start(bf16[1,128,384]{1,2,0:T(8,128)(2,1)} %copy.80) | copy-start | bytes 294916
  224.1 138.6 %all-reduce.5.cloned.1.call-start = ((), (), s32[]{:S(2)}) async-start(), calls=%async_computation.6 | async-start | bytes 1572864 | tf_op jit(solution)/shard_map/psum | solution.py:85
  274.6 1.8 copy-start.5
  276.4 1.2 copy-start.3
  276.4 2.5 copy-start.12
  277.6 6.7 %collective-permute-start.1 = (bf16[128,768]{1,0:T(8,128)(2,1)}, bf16[128,768]{1,0:T(8,128)(2,1)}, u32[]{:S(2)}, u32[]{:S(2)}) collective-permute-start(bf16[128,768]{1,0:T(8,128)(2,1)} %fusion.82), channel_id=1, source_target_pairs={{128,0},{129,1},{130,2},{131,3},{132,4},{133,5},{134,6},{135,7},{1... | collective-permute-start | bytes 589832 | tf_op jit(solution)/shard_map/ppermute | solution.py:13
  295.9 0.9 copy-start.1
  296.8 2.2 copy-start.9
  297.4 1.8 copy-start.14
  297.5 1.8 copy-start.15
  297.5 3.0 copy-start.13
  302.4 6.4 %copy-start.2 = (bf16[128,3072]{1,0:T(8,128)(2,1)S(1)}, bf16[128,3072]{1,0:T(8,128)(2,1)}, u32[]{:S(2)}) copy-start(bf16[128,3072]{1,0:T(8,128)(2,1)} %copy-done.1) | copy-start | bytes 2359300
  302.4 6.4 %copy-start.10 = (bf16[3,128,128]{2,1,0:T(8,128)(2,1)S(1)}, bf16[3,128,128]{2,1,0:T(8,128)(2,1)}, u32[]{:S(2)}) copy-start(bf16[3,128,128]{2,1,0:T(8,128)(2,1)} %convolution_convert_fusion.2) | copy-start | bytes 294916
  308.8 186.5 %reduce-scatter.7.cloned.1.call-start = ((), (), s32[]{:S(2)}) async-start(), calls=%async_computation.7 | async-start | bytes 9732096
  362.7 1.4 copy-start.4
Sparse Core Ops, SparseCore 0:
  10.6 76.7 all-gather.2
  90.0 53.5 all-gather.4
  147.4 27.3 reduce-scatter.4
  224.2 50.2 all-reduce.2
  308.9 53.7 all-reduce.4
  366.6 128.6 reduce-scatter.6
where the time goes:
time: 507 us; the launch traced here: 506 us
  waiting for transfers between devices  339 us (67%)
  blocking collectives  50.9 us (10%)
  matrix products  47.2 us (9%)
  local copies, waits for them, and re-layouts  29.4 us (6%)
  other arithmetic  20.8 us (4%)
  between operations  15.1 us (3%)
    unnamed x7, waiting for transfers between devices  130 us
    psum x2, waiting for transfers between devices, layer_backward(): lax.psum(norm_part.astype(jnp.bfloat16), 'tensor').astype(jnp.float32)  78.4 us
    all_gather x1, waiting for transfers between devices, local(): lax.all_gather(qkv_weight, 'fsdp', axis=2, tiled=True)  64.4 us
    all_gather x1, waiting for transfers between devices, local(): lax.all_gather(out_weight, 'fsdp', axis=2, tiled=True)  50.7 us
    all_gather x2, blocking collectives, layer_forward(): whole = lax.all_gather(hidden_own, 'tensor', axis=1, tiled=True)  25.5 us
    all_gather x2, blocking collectives, layer_backward(): whole_grad = lax.all_gather(grad_own, 'tensor', axis=1, tiled=True)  25.5 us
    unnamed x36, local copies, waits for them, and re-layouts  15.6 us
    dot_general x2, matrix products, layer_backward(): jnp.einsum('crh,cdh->rd', grad_qkv, w_qkv, preferred_element_type=jnp.flo...  12.7 us
  transfers between devices with their start and end apart: 8, of which 7 were waited for; matrix products, arithmetic and copies ran while one was open for 8% of the time, Pallas kernels for 0%

commit v1 on v0

--- a/solution.py
+++ b/solution.py
@@ -100,7 +100,9 @@
     live_keys = jnp.arange(length, dtype=jnp.int32)[None, :] < lengths[:, None]
     live_rows = live_keys.reshape(frame_rows, 1).astype(jnp.float32)
     gathered = (
-        lax.all_gather(qkv_weight, "fsdp", axis=2, tiled=True),
+        jnp.concatenate(
+            lax.all_to_all(jnp.stack([qkv_weight] * lax.axis_size("fsdp")), "fsdp", 0, 0), axis=2
+        ),
         lax.all_gather(out_weight, "fsdp", axis=2, tiled=True),
     )
     w_qkv = gathered[0][0]

time: 507 us -> 566 us (1.12)
  waiting for transfers between devices: 339 us -> 377 us
  starting transfers between devices: 3.49 us -> 17.7 us
  local copies, waits for them, and re-layouts: 29.4 us -> 40.2 us
    all_to_all x0 -> x1, waiting for transfers between devices: none -> 155 us  [local(): lax.all_to_all(jnp.stack([qkv_weight] * lax.axis_size('fsdp')), 'fsdp', 0...]
    all_gather x1 -> x0, waiting for transfers between devices: 64.4 us -> none  [local(): lax.all_gather(qkv_weight, 'fsdp', axis=2, tiled=True)]
    all_gather x1, waiting for transfers between devices: 50.7 us -> 0.02 us  [local(): lax.all_gather(out_weight, 'fsdp', axis=2, tiled=True)]
    all_to_all x0 -> x1, starting transfers between devices: none -> 12.9 us  [local(): lax.all_to_all(jnp.stack([qkv_weight] * lax.axis_size('fsdp')), 'fsdp', 0...]
    unnamed x36 -> x38, local copies, waits for them, and re-layouts: 15.6 us -> 17.9 us
    unnamed x7 -> x6, waiting for transfers between devices: 130 us -> 130 us
  transfers between devices with their start and end apart: 8 -> 8, of which waited for: 7 -> 7; matrix products, arithmetic and copies ran while one was open for 8% -> 7% of each run, Pallas kernels for 0% -> 0%
where the time goes in v1:
time: 566 us; the launch traced here: 564 us
  waiting for transfers between devices  377 us (67%)
  blocking collectives  49.4 us (9%)
  matrix products  44.1 us (8%)
  local copies, waits for them, and re-layouts  40.2 us (7%)
  other arithmetic  20.8 us (4%)
  starting transfers between devices  17.7 us (3%)
  between operations  14.8 us (3%)
    all_to_all x1, waiting for transfers between devices, local(): lax.all_to_all(jnp.stack([qkv_weight] * lax.axis_size('fsdp')), 'fsdp', 0...  155 us
    unnamed x6, waiting for transfers between devices  130 us
    psum x2, waiting for transfers between devices, layer_backward(): lax.psum(norm_part.astype(jnp.bfloat16), 'tensor').astype(jnp.float32)  76.5 us
    all_gather x2, blocking collectives, layer_backward(): whole_grad = lax.all_gather(grad_own, 'tensor', axis=1, tiled=True)  25.4 us
    all_gather x2, blocking collectives, layer_forward(): whole = lax.all_gather(hidden_own, 'tensor', axis=1, tiled=True)  24 us
    unnamed x38, local copies, waits for them, and re-layouts  17.9 us
    all_to_all x1, starting transfers between devices, local(): lax.all_to_all(jnp.stack([qkv_weight] * lax.axis_size('fsdp')), 'fsdp', 0...  12.9 us
    dot_general x2, matrix products, layer_backward(): jnp.einsum('crh,cdh->rd', grad_qkv, w_qkv, preferred_element_type=jnp.flo...  12.7 us
  transfers between devices with their start and end apart: 8, of which 7 were waited for; matrix products, arithmetic and copies ran while one was open for 7% of the time, Pallas kernels for 0%

profile of v1, /device:TPU:1, one launch (start us, length us, event | category | flops | bytes accessed | tf_op | source)
XLA Modules:
  0.0 564.3 jit_solution(11762694539593623710)
XLA Ops:
  7.2 4.5 stack.18
  11.6 12.9 %all-to-all-start = ((bf16[32,1,3,96,384]{4,3,2,1,0:T(8,128)(2,1)}), bf16[32,1,3,96,384]{4,3,2,1,0:T(8,128)(2,1)}, u32[]{:S(2)}, u32[]{:S(2)}) async-start(bf16[32,1,3,96,384]{4,3,2,1,0:T(8,128)(2,1)} %stack.18), calls=%async_computation | async-start | bytes 14155776 | tf_op jit(solution)/shard_map/all_to_all | solution.py:104
  24.6 0.7 all-gather.2.cloned.1.call-update
  26.0 12.4 %all_gather.15 = bf16[128,3072]{1,0:T(8,128)(2,1)S(1)} all-gather(bf16[128,768]{1,0:T(8,128)(2,1)S(1)} %copy-done.8), channel_id=1, replica_groups=mesh['section'=2,'fsdp'=32,'tensor'=4] {'tensor'}, dimensions={1}, use_global_device_ids=true | all-gather | bytes 983040 | tf_op jit(solution)/shard_map/all_gather | solution.py:34
  38.6 0.4 fusion.17
  39.0 155.2 %all-to-all-done = bf16[32,1,3,96,384]{4,3,2,1,0:T(8,128)(2,1)} async-done(((bf16[32,1,3,96,384]{4,3,2,1,0:T(8,128)(2,1)}), bf16[32,1,3,96,384]{4,3,2,1,0:T(8,128)(2,1)}, u32[]{:S(2)}, u32[]{:S(2)}) %all-to-all-start) | async-done | bytes 7077920 | tf_op jit(solution)/shard_map/all_to_all | solution.py:104
  194.2 3.9 copy.73
  198.2 1.2 fusion.21
  199.4 1.7 copy-done
  201.5 0.3 fusion.96
  201.8 0.2 fusion.30
  202.3 3.7 fusion.10
  206.1 0.8 copy-done.7
  206.9 14.7 %all_gather.18 = bf16[128,3072]{1,0:T(8,128)(2,1)S(1)} all-gather(bf16[128,768]{1,0:T(8,128)(2,1)S(1)} %copy-done.7), channel_id=1, replica_groups=mesh['section'=2,'fsdp'=32,'tensor'=4] {'tensor'}, dimensions={1}, use_global_device_ids=true | all-gather | bytes 983040 | tf_op jit(solution)/shard_map/all_gather | solution.py:60
  221.7 12.2 %reduce-scatter.5.cloned.1.call-done = f32[128,768]{1,0:T(8,128)} async-done(((f32[128,3072]{1,0:T(8,128)}), f32[128,768]{1,0:T(8,128)}) %reduce-scatter.5.cloned.1.call-update) | async-done | bytes 393232 | tf_op jit(solution)/shard_map/reduce_scatter | solution.py:52
  233.9 1.8 add_convert_fusion
  235.7 3.3 collective-permute-start
  239.0 1.3 fusion.35
  240.3 1.6 copy.84
  241.9 0.2 collective-permute-done
  242.2 11.6 %all_gather.17 = bf16[128,3072]{1,0:T(8,128)(2,1)S(1)} all-gather(bf16[128,768]{1,0:T(8,128)(2,1)S(1)} %broadcast_select_fusion.1), channel_id=1, replica_groups=mesh['section'=2,'fsdp'=32,'tensor'=4] {'tensor'}, dimensions={1}, use_global_device_ids=true | all-gather | bytes 983040 | tf_op jit(solution)/shard_map/all_gather | solution.py:34
  254.0 0.4 fusion.16
  254.3 4.3 fusion.22
  258.6 0.7 fusion.94
  259.3 1.0 copy.85
  260.3 1.7 copy.81
  262.0 0.7 copy.80
  262.7 1.8 fusion.98
  264.6 2.5 fusion.97
  267.0 2.1 convolution_convert_fusion.8
  269.1 2.1 convolution_convert_fusion.10
  271.2 2.1 convolution_convert_fusion.9
  273.3 1.0 copy.93
  274.3 1.6 copy.92
  276.0 1.6 copy.91
  277.6 6.4 %fusion.4 = bf16[128,3072]{1,0:T(8,128)(2,1)} fusion(bf16[3,3072,384]{2,1,0:T(8,128)(2,1)} %bitcast.130, bf16[1,128,384]{2,1,0:T(8,128)(2,1)S(1)} %copy.93, bf16[1,128,384]{2,1,0:T(8,128)(2,1)} %copy.92, bf16[1,128,384]{2,1,0:T(8,128)(2,1)} %copy.91), kind=kOutput, calls=%fused_computation.9 | convolution fusion | flops 906657792 | bytes 8159232 | tf_op jit(solution)/shard_map/crh,cdh->rd/dot_general | solution.py:83
  284.1 49.2 %all-reduce.3.cloned.1.call-done = bf16[128,3072]{1,0:T(8,128)(2,1)} async-done(((bf16[128,3072]{1,0:T(8,128)(2,1)}), bf16[128,3072]{1,0:T(8,128)(2,1)}) %all-reduce.3.cloned.1.call-update) | async-done | bytes 786448 | tf_op jit(solution)/shard_map/psum | solution.py:85
  333.3 1.8 convert_reduce_fusion.3
  335.3 1.0 fusion.54
  336.3 1.3 collective-permute-start.1
  337.6 2.0 convolution_convert_fusion.4
  339.6 3.5 collective-permute-done.1
  343.1 0.9 broadcast_select_fusion
  344.0 10.7 %all_gather.19 = bf16[128,3072]{1,0:T(8,128)(2,1)S(1)} all-gather(bf16[128,768]{1,0:T(8,128)(2,1)S(1)} %broadcast_select_fusion), channel_id=1, replica_groups=mesh['section'=2,'fsdp'=32,'tensor'=4] {'tensor'}, dimensions={1}, use_global_device_ids=true | all-gather | bytes 983040 | tf_op jit(solution)/shard_map/all_gather | solution.py:60
  354.7 0.9 copy-done.2
  355.6 0.6 fusion.38
  356.4 1.4 convolution_convert_fusion.5
  358.0 1.2 convolution_convert_fusion.7
  359.3 1.3 convolution_convert_fusion.6
  360.9 6.2 %fusion.5 = bf16[128,3072]{1,0:T(8,128)(2,1)} fusion(bf16[3,3072,384]{2,1,0:T(8,128)(2,1)} %bitcast.131, bf16[1,128,384]{2,1,0:T(8,128)(2,1)S(1)} %copy.102, bf16[1,128,384]{2,1,0:T(8,128)(2,1)S(1)} %copy.101, bf16[1,128,384]{2,1,0:T(8,128)(2,1)S(1)} %copy.100), kind=kOutput, calls=%fused_computation.10 | convolution fusion | flops 906657792 | bytes 8159232 | tf_op jit(solution)/shard_map/crh,cdh->rd/dot_general | solution.py:83
  367.5 0.8 copy-done.3
  368.3 0.8 convolution_convert_fusion.1
  369.1 2.1 convolution_convert_fusion
  371.2 10.1 %pad_maximum_fusion = bf16[3072,1536]{0,1:T(8,128)(2,1)} fusion(bf16[3072,384]{0,1:T(8,128)(2,1)S(1)} %convolution_convert_fusion.1, bf16[3072,1152]{0,1:T(8,128)(2,1)S(1)} %convolution_convert_fusion), kind=kLoop, calls=%fused_computation.5 | loop fusion | flops 18874368 | bytes 18874368 | tf_op jit(solution)/shard_map/concatenate | solution.py:128
  381.4 12.6 %copy.123 = bf16[3072,1536]{1,0:T(8,128)(2,1)} copy(bf16[3072,1536]{0,1:T(8,128)(2,1)} %pad_maximum_fusion) | data formatting | bytes 18874368
  394.0 27.3 %all-reduce.5.cloned.1.call-done = bf16[128,3072]{1,0:T(8,128)(2,1)} async-done(((bf16[128,3072]{1,0:T(8,128)(2,1)}), bf16[128,3072]{1,0:T(8,128)(2,1)}) %all-reduce.5.cloned.1.call-update) | async-done | bytes 786448 | tf_op jit(solution)/shard_map/psum | solution.py:85
  421.3 1.4 convert_element_type.235
  422.7 0.6 convert_reduce_fusion.2
  423.3 1.8 fusion.70
  425.2 128.9 %reduce-scatter.7.cloned.1.call-done = bf16[96,1536]{1,0:T(8,128)(2,1)} async-done(((bf16[3072,1536]{1,0:T(8,128)(2,1)}), bf16[96,1536]{1,0:T(8,128)(2,1)}) %reduce-scatter.7.cloned.1.call-update) | async-done | bytes 294928
  554.0 0.9 slice.53
  555.0 0.7 copy.106
  555.8 1.0 slice.52
  557.0 0.9 copy.105
  (67 shorter events, 2.9 us)
Async XLA Ops:
  11.6 14.4 %copy-start.8 = (bf16[128,768]{1,0:T(8,128)(2,1)S(1)}, bf16[128,768]{1,0:T(8,128)(2,1)}, u32[]{:S(2)}) copy-start(bf16[128,768]{1,0:T(8,128)(2,1)} %param.5) | copy-start | bytes 589828
  11.6 182.6 %all-to-all-start = ((bf16[32,1,3,96,384]{4,3,2,1,0:T(8,128)(2,1)}), bf16[32,1,3,96,384]{4,3,2,1,0:T(8,128)(2,1)}, u32[]{:S(2)}, u32[]{:S(2)}) async-start(bf16[32,1,3,96,384]{4,3,2,1,0:T(8,128)(2,1)} %stack.18), calls=%async_computation | async-start | bytes 14155776 | tf_op jit(solution)/shard_map/all_to_all | solution.py:104
  24.6 177.7 %all-gather.2.cloned.1.call-start = ((), (), s32[]{:S(2)}) async-start(), calls=%async_computation.3 | async-start | bytes 2433024 | tf_op jit(solution)/shard_map/all_gather | solution.py:106
  25.3 208.6 %reduce-scatter.5.cloned.1.call-start = ((), (), s32[]{:S(2)}) async-start(), calls=%async_computation.4 | async-start | bytes 1966080 | tf_op jit(solution)/shard_map/reduce_scatter | solution.py:52
  198.2 2.9 copy-start
  206.0 0.9 copy-start.7
  206.0 33.0 %copy-start.1 = (bf16[1,384,3072]{1,2,0:T(8,128)(2,1)S(1)}, bf16[1,384,3072]{1,2,0:T(8,128)(2,1)}, u32[]{:S(2)}) copy-start(bf16[1,384,3072]{1,2,0:T(8,128)(2,1)} %all-gather.2.cloned.1.call-done) | copy-start | bytes 7077892
  206.0 127.3 %all-reduce.3.cloned.1.call-start = ((), (), s32[]{:S(2)}) async-start(), calls=%async_computation.5 | async-start | bytes 1572864 | tf_op jit(solution)/shard_map/psum | solution.py:85
  235.7 6.4 %collective-permute-start = (bf16[128,768]{1,0:T(8,128)(2,1)}, bf16[128,768]{1,0:T(8,128)(2,1)}, u32[]{:S(2)}, u32[]{:S(2)}) collective-permute-start(bf16[128,768]{1,0:T(8,128)(2,1)} %add_convert_fusion), channel_id=1, source_target_pairs={{0,128},{1,129},{2,130},{3,131},{4,132},{5,133},{6,134},{7,135},{8... | collective-permute-start | bytes 589832 | tf_op jit(solution)/shard_map/ppermute | solution.py:13
  260.3 77.3 %copy-start.9 = (bf16[1,128,384]{1,2,0:T(8,128)(2,1)}, bf16[1,128,384]{1,2,0:T(8,128)(2,1)S(1)}, u32[]{:S(2)}) copy-start(bf16[1,128,384]{1,2,0:T(8,128)(2,1)S(1)} %copy.85) | copy-start | bytes 294916
  262.7 8.5 %copy-start.12 = (bf16[1,128,384]{1,2,0:T(8,128)(2,1)S(1)}, bf16[1,128,384]{1,2,0:T(8,128)(2,1)}, u32[]{:S(2)}) copy-start(bf16[1,128,384]{1,2,0:T(8,128)(2,1)} %copy.81) | copy-start | bytes 294916
  284.1 137.3 %all-reduce.5.cloned.1.call-start = ((), (), s32[]{:S(2)}) async-start(), calls=%async_computation.6 | async-start | bytes 1572864 | tf_op jit(solution)/shard_map/psum | solution.py:85
  333.3 1.8 copy-start.6
  335.1 1.2 copy-start.4
  335.2 2.5 copy-start.13
  336.3 6.7 %collective-permute-start.1 = (bf16[128,768]{1,0:T(8,128)(2,1)}, bf16[128,768]{1,0:T(8,128)(2,1)}, u32[]{:S(2)}, u32[]{:S(2)}) collective-permute-start(bf16[128,768]{1,0:T(8,128)(2,1)} %fusion.54), channel_id=1, source_target_pairs={{128,0},{129,1},{130,2},{131,3},{132,4},{133,5},{134,6},{135,7},{1... | collective-permute-start | bytes 589832 | tf_op jit(solution)/shard_map/ppermute | solution.py:13
  354.7 0.9 copy-start.2
  355.6 2.2 copy-start.10
  356.2 1.8 copy-start.15
  356.2 1.8 copy-start.16
  356.2 3.0 copy-start.14
  367.2 1.1 copy-start.3
  367.2 1.1 copy-start.11
  367.5 186.6 %reduce-scatter.7.cloned.1.call-start = ((), (), s32[]{:S(2)}) async-start(), calls=%async_computation.7 | async-start | bytes 9732096
  421.3 1.4 copy-start.5
Sparse Core Ops, SparseCore 0:
  28.0 102.6 all-gather.1
  206.2 27.6 reduce-scatter.4
  284.2 49.0 all-reduce.2
  367.6 53.7 all-reduce.4
  425.2 128.7 reduce-scatter.6
